TPU v7x, 32 devices: a whole 2x2x4 slice. The times are simulated.
32 devices in a mesh: blk: 16 (over z, x, core), ep: 2 (over y).
Axes of the slice: x: 2, y: 2, z: 4, core: 2. Of those that a mesh axis runs over, the one named last changes fastest.
Arguments:
- hidden_in: bfloat16 [256, 4096], P('blk'), may hold values from -6 to 6
- out_grad: bfloat16 [256, 4096], P('blk'), may hold values from -6 to 6
- expert_ids: int32 [256, 2], P('blk'), may hold values from 0 to 3, all different within a row; in each aligned block of 16 rows (0 to 15, 16 to 31, ...) at most 12 rows name the same one
- gate_values: bfloat16 [256, 2], P('blk'), may hold values from 0.099609375 to 1
- w_gate: bfloat16 [4, 14336, 4096], P('ep', 'blk'), may hold values from -0.09375 to 0.09375
- w_up: bfloat16 [4, 14336, 4096], P('ep', 'blk'), may hold values from -0.09375 to 0.09375
- w_down: bfloat16 [4, 14336, 4096], P('ep', 'blk'), may hold values from -0.046875 to 0.046875
Outputs:
- input_grad: bfloat16 [256, 4096], P('blk')
- gate_grad: float32 [256, 2], P('blk')
- grad_gate: bfloat16 [4, 14336, 4096], P('ep', 'blk')
- grad_up: bfloat16 [4, 14336, 4096], P('ep', 'blk')
- grad_down: bfloat16 [4, 14336, 4096], P('ep', 'blk')
Inputs may be any that keep to these rules, and one draw needn't show every extreme that they name: `expert_ids`: each row names 2 different experts; in each aligned block of 16 rows (the rows of one device) no expert is named by more than 12 rows, a bound that some block reaches.
All inputs are finite; a program needn't handle non-finite values.
Results may differ from a plain program's by a relative error of at most 0.008.
Values may be sent and summed in bfloat16 or wider, within the bound.
A program may use at most 256 MiB of HBM per device.

v0:
```python
import functools

import jax
import jax.numpy as jnp
from jax import lax
from jax.experimental import pallas as pl
from jax.experimental.pallas import tpu as pltpu
from jax.sharding import PartitionSpec as P

MESH = pl.DeviceIdType.MESH
CHUNKS = 4
VMEM_LIMIT = 62 * 1024 * 1024


def greet(blk_peers, ep_peers):
    barrier = pltpu.get_barrier_semaphore()
    for peer in blk_peers:
        pl.semaphore_signal(barrier, inc=1, device_id={"blk": peer}, device_id_type=MESH)
    for peer in ep_peers:
        pl.semaphore_signal(barrier, inc=1, device_id={"ep": peer}, device_id_type=MESH)
    pl.semaphore_wait(barrier, len(blk_peers) + len(ep_peers))


def forward_kernel(
    n, x_in, dy_in, w_in, w_gate, w_up, w_down,
    x_all, dy_all, dg_t, du_t, aw_t, sg,
    w_all, wbuf, acc, wsem, own_sem, send_sem, recv_sem, fsend_sem, frecv_sem,
    wsend_sem, wrecv_sem, wfsend_sem, wfrecv_sem,
):
    experts, hidden, width = w_gate.shape
    tb, tokens = x_in.shape[0], x_all.shape[0]
    chunks, half = CHUNKS, n // 2
    dc = width // chunks
    mats = (w_gate, w_up, w_down)
    kinds = ((x_in, x_all), (dy_in, dy_all))
    me = lax.axis_index("blk")
    partner = me + 1 - 2 * lax.rem(me, 2)

    def cols(c):
        return pl.ds(pl.multiple_of(c * dc, dc), dc)

    def rows(o):
        return pl.ds(pl.multiple_of(o * tb, tb), tb)

    def tile(c, e, m):
        slot = e * 3 + m
        return pltpu.make_async_copy(mats[m].at[e, :, cols(c)], wbuf.at[slot], wsem.at[slot])

    for e in range(experts):
        for m in range(3):
            tile(0, e, m).start()
    own = [
        pltpu.make_async_copy(x_in, x_all.at[rows(me)], own_sem.at[0]),
        pltpu.make_async_copy(dy_in, dy_all.at[rows(me)], own_sem.at[1]),
        pltpu.make_async_copy(w_in, w_all.at[me], own_sem.at[2]),
    ]
    for copy in own:
        copy.start()

    greet([partner] + [lax.rem(me + 2 * k, n) for k in range(1, half)], [])

    def remote(src, dst, ssem, rsem, to):
        return pltpu.make_async_remote_copy(
            src_ref=src, dst_ref=dst, send_sem=ssem, recv_sem=rsem,
            device_id={"blk": to}, device_id_type=MESH,
        )

    def send(i, c, k):
        src, dst = kinds[i]
        return remote(
            src.at[:, cols(c)], dst.at[rows(me), cols(c)],
            send_sem.at[i, c, k], recv_sem.at[i, c, k], lax.rem(me + 2 * k, n),
        )

    def arrive(i, c, k):
        dst = kinds[i][1].at[rows(lax.rem(me + n - 2 * k, n)), cols(c)]
        return remote(dst, dst, send_sem.at[i, c, k], recv_sem.at[i, c, k], lax.rem(me + 2 * k, n))

    def pass_own(i, c):
        src, dst = kinds[i]
        return remote(
            src.at[:, cols(c)], dst.at[rows(me), cols(c)],
            fsend_sem.at[i, c, 0], frecv_sem.at[i, c, 0], partner,
        )

    def pass_on(i, c, k):
        dst = kinds[i][1].at[rows(lax.rem(me + n - 2 * k, n)), cols(c)]
        return remote(dst, dst, fsend_sem.at[i, c, k], frecv_sem.at[i, c, k], partner)

    def passed(i, c, k):
        dst = kinds[i][1].at[rows(lax.rem(partner + n - 2 * k, n)), cols(c)]
        return remote(dst, dst, fsend_sem.at[i, c, k], frecv_sem.at[i, c, k], partner)

    def wsend(k):
        return remote(w_in, w_all.at[me], wsend_sem.at[k], wrecv_sem.at[k], lax.rem(me + 2 * k, n))

    def warrive(k):
        dst = w_all.at[lax.rem(me + n - 2 * k, n)]
        return remote(dst, dst, wsend_sem.at[k], wrecv_sem.at[k], lax.rem(me + 2 * k, n))

    def wpass_own():
        return remote(w_in, w_all.at[me], wfsend_sem.at[0], wfrecv_sem.at[0], partner)

    def wpass_on(k):
        dst = w_all.at[lax.rem(me + n - 2 * k, n)]
        return remote(dst, dst, wfsend_sem.at[k], wfrecv_sem.at[k], partner)

    def wpassed(k):
        dst = w_all.at[lax.rem(partner + n - 2 * k, n)]
        return remote(dst, dst, wfsend_sem.at[k], wfrecv_sem.at[k], partner)

    @pl.loop(0, chunks)
    def _(c):
        for i in range(2):
            pass_own(i, c).start()

        @pl.loop(1, half)
        def _(k):
            for i in range(2):
                send(i, c, k).start()

    wpass_own().start()

    @pl.loop(1, half)
    def _(k):
        wsend(k).start()

    acc[...] = jnp.zeros_like(acc)
    for copy in own:
        copy.wait()

    @pl.loop(0, chunks)
    def _(c):
        @pl.loop(1, half)
        def _(k):
            for i in range(2):
                arrive(i, c, k).wait_recv()
                pass_on(i, c, k).start()

        @pl.loop(0, half)
        def _(k):
            for i in range(2):
                passed(i, c, k).wait_recv()

        @pl.loop(0, experts)
        def _(e):
            for m in range(3):
                slot = e * 3 + m
                tile(c, e, m).wait()
                right = (x_all, x_all, dy_all)[m][:, cols(c)]
                acc[slot] += lax.dot_general(
                    wbuf[slot], right, (((1,), (1,)), ((), ())),
                    preferred_element_type=jnp.float32,
                )

                @pl.when(c + 1 < chunks)
                def _():
                    tile(c + 1, e, m).start()

    @pl.loop(1, half)
    def _(k):
        warrive(k).wait_recv()
        wpass_on(k).start()

    @pl.loop(0, half)
    def _(k):
        wpassed(k).wait_recv()

    weights = jnp.sum(w_all[...], axis=0)
    strip = 32
    sg[...] = jnp.zeros_like(sg)
    for e in range(experts):
        weight = weights[e : e + 1, :]

        def body(r, total):
            part = pl.ds(pl.multiple_of(r * strip, strip), strip)
            gate, up, back = acc[e * 3, part], acc[e * 3 + 1, part], acc[e * 3 + 2, part]
            sig = jax.nn.sigmoid(gate)
            silu = gate * sig
            act = silu * up
            dact = weight * back
            du_t[e, part] = (dact * silu).astype(jnp.bfloat16)
            dg_t[e, part] = (dact * up * sig * (1.0 + gate * (1.0 - sig))).astype(jnp.bfloat16)
            aw_t[e, part] = (act * weight).astype(jnp.bfloat16)
            return total + jnp.sum(act * back, axis=0, keepdims=True)

        sg[e : e + 1, :] = lax.fori_loop(
            0, hidden // strip, body, jnp.zeros((1, tokens), jnp.float32)
        )

    @pl.loop(0, chunks)
    def _(c):
        for i in range(2):
            pass_own(i, c).wait_send()

        @pl.loop(1, half)
        def _(k):
            for i in range(2):
                send(i, c, k).wait_send()
                pass_on(i, c, k).wait_send()

    wpass_own().wait_send()

    @pl.loop(1, half)
    def _(k):
        wsend(k).wait_send()
        wpass_on(k).wait_send()


def grads_kernel(dg_t, du_t, aw_t, x, dy, out_g, out_u, out_d):
    for left, right, out in ((dg_t, x, out_g), (du_t, x, out_u), (aw_t, dy, out_d)):
        out[0] = jnp.dot(left[0], right[...], preferred_element_type=jnp.float32).astype(out.dtype)


def back_kernel(
    n, ne, dgu, sg, w_gate, w_up, out, gate_out,
    wbuf, acc, part, rbuf, csum, gbuf, ebuf, s_r, s_c, s_g,
    wsem, psend, precv, csend, crecv, esend, erecv,
):
    experts, hidden, width = w_gate.shape
    chunks, half = CHUNKS, n // 2
    dc = width // chunks
    tb = out.shape[0]
    me, ep = lax.axis_index("blk"), lax.axis_index("ep")
    core = lax.rem(me, 2)
    chip = me // 2
    partner = me + 1 - 2 * core
    mats = (w_gate, w_up)
    f32, bf16 = jnp.float32, jnp.bfloat16

    def cols(c):
        return pl.ds(pl.multiple_of(c * dc, dc), dc)

    def rows(q):
        return pl.ds(pl.multiple_of(q * tb, tb), tb)

    def tile(c, e, m):
        slot = e * 2 + m
        return pltpu.make_async_copy(mats[m].at[e, :, cols(c)], wbuf.at[slot], wsem.at[slot])

    def remote(src, dst, ssem, rsem, **to):
        return pltpu.make_async_remote_copy(
            src_ref=src, dst_ref=dst, send_sem=ssem, recv_sem=rsem,
            device_id=to, device_id_type=MESH,
        )

    def to_partner(c):
        return remote(part.at[c, 1 - core], rbuf.at[c], psend.at[c], precv.at[c], blk=partner)

    def to_chip(c, k):
        q = lax.rem(chip + k, half)
        return remote(
            csum.at[c, rows(q)], gbuf.at[c, k], csend.at[c, k], crecv.at[c, k], blk=2 * q + core
        )

    def to_ep(c, k):
        return remote(
            ebuf.at[c, ep], ebuf.at[c, ep], esend.at[c, k], erecv.at[c, k], ep=lax.rem(ep + k, ne)
        )

    def from_ep(c, k):
        dst = ebuf.at[c, lax.rem(ep + ne - k, ne)]
        return remote(dst, dst, esend.at[c, k], erecv.at[c, k], ep=lax.rem(ep + k, ne))

    def g_partner():
        return remote(sg, s_r, psend.at[chunks], precv.at[chunks], blk=partner)

    def g_chip(k):
        q = lax.rem(chip + k, half)
        return remote(s_c, s_g.at[k], csend.at[chunks, k], crecv.at[chunks, k], blk=2 * q + core)

    def g_ep(k):
        return remote(
            gate_out.at[ep], gate_out.at[ep], esend.at[chunks, k], erecv.at[chunks, k],
            ep=lax.rem(ep + k, ne),
        )

    def g_from_ep(k):
        dst = gate_out.at[lax.rem(ep + ne - k, ne)]
        return remote(
            dst, dst, esend.at[chunks, k], erecv.at[chunks, k], ep=lax.rem(ep + k, ne)
        )

    for e in range(experts):
        for m in range(2):
            tile(0, e, m).start()
    greet(
        [partner] + [lax.rem(me + 2 * k, n) for k in range(1, half)],
        [lax.rem(ep + k, ne) for k in range(1, ne)],
    )
    g_partner().start()

    @pl.loop(0, chunks + 3)
    def _(step):
        @pl.when(step < chunks)
        def _():
            c = step
            for e in range(experts):
                for m in range(2):
                    slot = e * 2 + m
                    tile(c, e, m).wait()
                    term = jnp.dot(dgu[e, m], wbuf[slot], preferred_element_type=f32)
                    if slot == 0:
                        acc[...] = term
                    else:
                        acc[...] += term

                    @pl.when(c + 1 < chunks)
                    def _():
                        tile(c + 1, e, m).start()

            for q in range(half):
                for p in range(2):
                    part[c, p, q * tb : (q + 1) * tb, :] = acc[
                        (2 * q + p) * tb : (2 * q + p + 1) * tb, :
                    ].astype(bf16)
            to_partner(c).start()

        @pl.when((step >= 1) & (step < chunks + 1))
        def _():
            c = step - 1
            to_partner(c).wait_recv()
            csum[c] = (part[c, core].astype(f32) + rbuf[c].astype(f32)).astype(bf16)

            @pl.loop(1, half)
            def _(k):
                to_chip(c, k).start()

        @pl.when(step == 1)
        def _():
            g_partner().wait_recv()
            s_c[...] = sg[...] + s_r[...]

            @pl.loop(1, half)
            def _(k):
                g_chip(k).start()

        @pl.when((step >= 2) & (step < chunks + 2))
        def _():
            c = step - 2

            @pl.loop(1, half)
            def _(k):
                to_chip(c, k).wait_recv()

            total = csum[c, rows(chip)].astype(f32)
            for k in range(1, half):
                total = total + gbuf[c, k].astype(f32)
            ebuf[c, ep] = total.astype(bf16)

            for k in range(1, ne):
                to_ep(c, k).start()

        @pl.when(step == 2)
        def _():
            @pl.loop(1, half)
            def _(k):
                g_chip(k).wait_recv()

            total = s_c[...]
            for k in range(1, half):
                total = total + s_g[k]
            gate_out[ep] = total
            for k in range(1, ne):
                g_ep(k).start()

        @pl.when(step >= 3)
        def _():
            c = step - 3
            for k in range(1, ne):
                from_ep(c, k).wait_recv()
            total = ebuf[c, 0].astype(f32)
            for k in range(1, ne):
                total = total + ebuf[c, k].astype(f32)
            out[:, cols(c)] = total.astype(bf16)

    for k in range(1, ne):
        g_from_ep(k).wait_recv()
        g_ep(k).wait_send()
    g_partner().wait_send()

    @pl.loop(1, half)
    def _(k):
        g_chip(k).wait_send()

    @pl.loop(0, chunks)
    def _(c):
        to_partner(c).wait_send()
        for k in range(1, ne):
            to_ep(c, k).wait_send()

        @pl.loop(1, half)
        def _(k):
            to_chip(c, k).wait_send()


def shards(n, ne, hidden_in, out_grad, expert_ids, gate_values, w_gate, w_up, w_down):
    tb, width = hidden_in.shape
    experts, hidden, _ = w_gate.shape
    tokens, half, chunks = tb * n, n // 2, CHUNKS
    dc = width // chunks
    me, ep = lax.axis_index("blk"), lax.axis_index("ep")
    f32, bf16 = jnp.float32, jnp.bfloat16
    lines = -(-experts // 8) * 8

    numbers = ep * experts + jnp.arange(lines, dtype=jnp.int32)
    held = (jnp.arange(lines) < experts)[:, None]
    weight = jnp.zeros((lines, tb), f32)
    for k in range(expert_ids.shape[1]):
        hit = (expert_ids[:, k][None, :] == numbers[:, None]) & held
        weight = weight + jnp.where(hit, gate_values[:, k].astype(f32)[None, :], 0.0)
    mine = (jnp.arange(tokens) // tb == me)[None, :]
    weight = jnp.where(mine, jnp.tile(weight, (1, n)), 0.0)

    any_spec = pl.BlockSpec(memory_space=pl.ANY)
    vmem_spec = pl.BlockSpec(memory_space=pltpu.VMEM)
    dma = pltpu.SemaphoreType.DMA
    x_all, dy_all, dg_t, du_t, aw_t, sg = pl.pallas_call(
        functools.partial(forward_kernel, n),
        out_shape=[
            jax.ShapeDtypeStruct((tokens, width), bf16),
            jax.ShapeDtypeStruct((tokens, width), bf16),
            jax.ShapeDtypeStruct((experts, hidden, tokens), bf16),
            jax.ShapeDtypeStruct((experts, hidden, tokens), bf16),
            jax.ShapeDtypeStruct((experts, hidden, tokens), bf16),
            jax.ShapeDtypeStruct((lines, tokens), f32),
        ],
        in_specs=[any_spec] * 6,
        out_specs=[vmem_spec] * 6,
        scratch_shapes=[
            pltpu.VMEM((n, lines, tokens), f32),
            pltpu.VMEM((3 * experts, hidden, dc), bf16),
            pltpu.VMEM((3 * experts, hidden, tokens), f32),
            dma((3 * experts,)),
            dma((3,)),
            dma((2, chunks, half)),
            dma((2, chunks, half)),
            dma((2, chunks, half)),
            dma((2, chunks, half)),
            dma((half,)),
            dma((half,)),
            dma((half,)),
            dma((half,)),
        ],
        compiler_params=pltpu.CompilerParams(
            collective_id=0, has_side_effects=True, vmem_limit_bytes=VMEM_LIMIT
        ),
        name="gather_forward",
    )(hidden_in, out_grad, weight, w_gate, w_up, w_down)

    dgu = jnp.swapaxes(jnp.stack([dg_t, du_t], axis=1), 2, 3)
    input_grad, gate_all = pl.pallas_call(
        functools.partial(back_kernel, n, ne),
        out_shape=[
            jax.ShapeDtypeStruct((tb, width), bf16),
            jax.ShapeDtypeStruct((ne, lines, tokens), f32),
        ],
        in_specs=[vmem_spec, vmem_spec, any_spec, any_spec],
        out_specs=[vmem_spec] * 2,
        scratch_shapes=[
            pltpu.VMEM((2 * experts, hidden, dc), bf16),
            pltpu.VMEM((tokens, dc), f32),
            pltpu.VMEM((chunks, 2, tokens // 2, dc), bf16),
            pltpu.VMEM((chunks, tokens // 2, dc), bf16),
            pltpu.VMEM((chunks, tokens // 2, dc), bf16),
            pltpu.VMEM((chunks, half, tb, dc), bf16),
            pltpu.VMEM((chunks, ne, tb, dc), bf16),
            pltpu.VMEM((lines, tokens), f32),
            pltpu.VMEM((lines, tokens), f32),
            pltpu.VMEM((half, lines, tokens), f32),
            dma((2 * experts,)),
            dma((chunks + 1,)),
            dma((chunks + 1,)),
            dma((chunks + 1, half)),
            dma((chunks + 1, half)),
            dma((chunks + 1, ne)),
            dma((chunks + 1, ne)),
        ],
        compiler_params=pltpu.CompilerParams(
            collective_id=1, has_side_effects=True, vmem_limit_bytes=VMEM_LIMIT
        ),
        name="back_scatter",
    )(dgu, sg, w_gate, w_up)

    wide = min(512, width)
    left = pl.BlockSpec((1, hidden, tokens), lambda e, d: (e, 0, 0))
    right = pl.BlockSpec((tokens, wide), lambda e, d: (0, d))
    result = pl.BlockSpec((1, hidden, wide), lambda e, d: (e, 0, d))
    grads = pl.pallas_call(
        grads_kernel,
        grid=(experts, width // wide),
        out_shape=[jax.ShapeDtypeStruct((experts, hidden, width), bf16)] * 3,
        in_specs=[left] * 3 + [right] * 2,
        out_specs=[result] * 3,
        compiler_params=pltpu.CompilerParams(vmem_limit_bytes=VMEM_LIMIT),
        name="weight_grads",
    )(dg_t, du_t, aw_t, x_all, dy_all)

    by_expert = gate_all[:, :experts].reshape(ne * experts, tokens)
    by_expert = lax.dynamic_slice_in_dim(by_expert, me * tb, tb, axis=1)
    hits = expert_ids[:, :, None] == jnp.arange(ne * experts)[None, None, :]
    gate_grad = jnp.sum(jnp.where(hits, by_expert.T[:, None, :], 0.0), axis=2)
    return (input_grad, gate_grad, *grads)


def solution(mesh):
    tok = P("blk", None)
    wts = P("ep", "blk", None)
    return jax.shard_map(
        functools.partial(shards, mesh.shape["blk"], mesh.shape["ep"]),
        mesh=mesh,
        in_specs=(tok,) * 4 + (wts,) * 3,
        out_specs=(tok,) * 2 + (wts,) * 3,
        check_vma=False,
    )
```

profile of v0, /device:TPU:0, one launch (start us, length us, event | category | flops | bytes accessed | tf_op | source)
XLA Modules:
  0.0 143.6 jit_solution(14654944322627141030)
XLA Ops:
  0.6 0.8 slice_bitcast_fusion.1
  1.4 0.7 bitcast_convert_fusion.1
  2.1 0.1 select_add_fusion
  2.2 0.1 tile.10
  2.3 0.6 broadcast_select_fusion.w_in
  2.9 66.2 %gather_forward.1 = (bf16[256,4096]{1,0:T(8,128)(2,1)}, bf16[256,4096]{1,0:T(8,128)(2,1)}, bf16[2,896,256]{2,1,0:T(8,128)(2,1)}, bf16[2,896,256]{2,1,0:T(8,128)(...) custom-call(bf16[16,4096]{1,0:T(8,128)(2,1)} %x_in.1, bf16[16,4096]{1,0:T(8,128)(2,1)} %dy_in.1, ...), custom_call_target="tpu_custom_call" | custom-call | tf_op jit(solution)/shard_map/gather_forward/pallas_call | solution.py:418
  69.2 22.6 %weight_grads.1 = (bf16[2,896,4096]{2,1,0:T(8,128)(2,1)}, bf16[2,896,4096]{2,1,0:T(8,128)(2,1)}, bf16[2,896,4096]{2,1,0:T(8,128)(2,1)}) custom-call(bf16[2,896,256]{2,1,0:T(8,128)(2,1)} %get-tuple-element.16.dg_t, bf16[2,896,256]{2,1,0:T(8,128)(2,1)} %get-tuple-element.17.du_t, bf16[2,896,256]{2,1,0:T(8,128)(2,1)} %get-tuple-element.21.aw_t, ...), custom_call_target="tpu_custom_call" | custom-call | tf_op jit(solution)/shard_map/weight_grads/pallas_call | solution.py:489
  91.8 1.5 %copy.16 = bf16[2,896,256]{1,2,0:T(8,128)(2,1)S(1)} copy(bf16[2,896,256]{2,1,0:T(8,128)(2,1)} %get-tuple-element.16.dg_t) | data formatting | bytes 1835008 | tf_op jit(solution)/shard_map/gather_forward/pallas_call | solution.py:418
  93.3 1.5 %copy.17 = bf16[2,896,256]{1,2,0:T(8,128)(2,1)S(1)} copy(bf16[2,896,256]{2,1,0:T(8,128)(2,1)} %get-tuple-element.17.du_t) | data formatting | bytes 1835008 | tf_op jit(solution)/shard_map/gather_forward/pallas_call | solution.py:418
  94.9 1.4 %maximum_bitcast_fusion.dgu = bf16[2,2,256,896]{3,2,1,0:T(8,128)(2,1)} fusion(bf16[2,1,896,256]{2,3,1,0:T(8,128)(2,1)S(1)} %bitcast.17, bf16[2,1,896,256]{2,3,1,0:T(8,128)(2,1)S(1)} %bitcast.16), kind=kLoop, calls=%fused_computation | loop fusion | flops 917504 | bytes 3670016 | tf_op jit(solution)/shard_map/transpose | solution.py:451
  96.3 0.0 copy-start
  96.3 44.3 %back_scatter.1 = (bf16[16,4096]{1,0:T(8,128)(2,1)}, f32[2,8,256]{2,1,0:T(8,128)}) custom-call(bf16[2,2,256,896]{3,2,1,0:T(8,128)(2,1)} %maximum_bitcast_fusion.dgu, f32[8,256]{1,0:T(8,128)} %get-tuple-element.18.sg, bf16[2,896,4096]{2,1,0:T(8,128)(2,1)} %w_gate.3, bf16[2,896,4096]{2,1,0:T(8,128)(2,1)} %w_up.3), custom_call_target="tpu_custom_call" | custom-call | tf_op jit(solution)/shard_map/back_scatter/pallas_call | solution.py:452
  140.6 0.7 slice.19
  141.3 0.1 dynamic-slice_bitcast_fusion
  141.4 0.0 copy-done
  141.4 0.6 select_reduce_fusion
  142.0 1.6 %copy.19 = bf16[16,4096]{1,0:T(8,128)(2,1)} copy(bf16[16,4096]{1,0:T(8,128)(2,1)} %get-tuple-element.36) | data formatting | bytes 262144
  (5 shorter events, 0.0 us)
Async XLA Ops:
  96.3 45.1 %copy-start = (s32[16,2]{0,1:T(2,128)S(1)}, s32[16,2]{0,1:T(2,128)}, u32[]{:S(2)}) copy-start(s32[16,2]{0,1:T(2,128)} %param.9) | copy-start | bytes 388
where the time goes:
time: 145 us; the launch traced here: 144 us
  Pallas kernels  133 us (92%)
  local copies, waits for them, and re-layouts  6.3 us (4%)
  other arithmetic  3.46 us (2%)
    pallas_call x1, Pallas kernels, shards(): pl.pallas_call(functools.partial(forward_kernel, n), out_shape=[jax.Shape...  66.2 us
    pallas_call x1, Pallas kernels, shards(): pl.pallas_call(functools.partial(back_kernel, n, ne), out_shape=[jax.Shap...  44.3 us
    pallas_call x1, Pallas kernels, shards(): pl.pallas_call(grads_kernel, grid=(experts, width // wide), out_shape=[ja...  22.6 us
    pallas_call x2, local copies, waits for them, and re-layouts, shards(): pl.pallas_call(functools.partial(forward_kernel, n), out_shape=[jax.Shape...  3.06 us

commit v1 on v0

--- a/solution.py
+++ b/solution.py
@@ -9,6 +9,7 @@
 
 MESH = pl.DeviceIdType.MESH
 CHUNKS = 4
+BACK_CHUNKS = 8
 VMEM_LIMIT = 62 * 1024 * 1024
 
 
@@ -24,17 +25,16 @@
 def forward_kernel(
     n, x_in, dy_in, w_in, w_gate, w_up, w_down,
     x_all, dy_all, dg_t, du_t, aw_t, sg,
-    w_all, wbuf, acc, wsem, own_sem, send_sem, recv_sem, fsend_sem, frecv_sem,
-    wsend_sem, wrecv_sem, wfsend_sem, wfrecv_sem,
+    w_all, wbuf, turned, acc, wsem, own_sem, zsend, zrecv, xsend, xrecv, csend, crecv,
 ):
     experts, hidden, width = w_gate.shape
     tb, tokens = x_in.shape[0], x_all.shape[0]
-    chunks, half = CHUNKS, n // 2
+    chunks, lines = CHUNKS, n // 4
     dc = width // chunks
     mats = (w_gate, w_up, w_down)
-    kinds = ((x_in, x_all), (dy_in, dy_all))
     me = lax.axis_index("blk")
     partner = me + 1 - 2 * lax.rem(me, 2)
+    across = me + 2 - 4 * lax.rem(me // 2, 2)
 
     def cols(c):
         return pl.ds(pl.multiple_of(c * dc, dc), dc)
@@ -57,7 +57,7 @@
     for copy in own:
         copy.start()
 
-    greet([partner] + [lax.rem(me + 2 * k, n) for k in range(1, half)], [])
+    greet([partner, across] + [lax.rem(me + 4 * k, n) for k in range(1, lines)], [])
 
     def remote(src, dst, ssem, rsem, to):
         return pltpu.make_async_remote_copy(
@@ -65,106 +65,142 @@
             device_id={"blk": to}, device_id_type=MESH,
         )
 
-    def send(i, c, k):
-        src, dst = kinds[i]
-        return remote(
-            src.at[:, cols(c)], dst.at[rows(me), cols(c)],
-            send_sem.at[i, c, k], recv_sem.at[i, c, k], lax.rem(me + 2 * k, n),
-        )
-
-    def arrive(i, c, k):
-        dst = kinds[i][1].at[rows(lax.rem(me + n - 2 * k, n)), cols(c)]
-        return remote(dst, dst, send_sem.at[i, c, k], recv_sem.at[i, c, k], lax.rem(me + 2 * k, n))
-
-    def pass_own(i, c):
-        src, dst = kinds[i]
-        return remote(
-            src.at[:, cols(c)], dst.at[rows(me), cols(c)],
-            fsend_sem.at[i, c, 0], frecv_sem.at[i, c, 0], partner,
-        )
-
-    def pass_on(i, c, k):
-        dst = kinds[i][1].at[rows(lax.rem(me + n - 2 * k, n)), cols(c)]
-        return remote(dst, dst, fsend_sem.at[i, c, k], frecv_sem.at[i, c, k], partner)
-
-    def passed(i, c, k):
-        dst = kinds[i][1].at[rows(lax.rem(partner + n - 2 * k, n)), cols(c)]
-        return remote(dst, dst, fsend_sem.at[i, c, k], frecv_sem.at[i, c, k], partner)
-
-    def wsend(k):
-        return remote(w_in, w_all.at[me], wsend_sem.at[k], wrecv_sem.at[k], lax.rem(me + 2 * k, n))
-
-    def warrive(k):
-        dst = w_all.at[lax.rem(me + n - 2 * k, n)]
-        return remote(dst, dst, wsend_sem.at[k], wrecv_sem.at[k], lax.rem(me + 2 * k, n))
-
-    def wpass_own():
-        return remote(w_in, w_all.at[me], wfsend_sem.at[0], wfrecv_sem.at[0], partner)
-
-    def wpass_on(k):
-        dst = w_all.at[lax.rem(me + n - 2 * k, n)]
-        return remote(dst, dst, wfsend_sem.at[k], wfrecv_sem.at[k], partner)
-
-    def wpassed(k):
-        dst = w_all.at[lax.rem(partner + n - 2 * k, n)]
-        return remote(dst, dst, wfsend_sem.at[k], wfrecv_sem.at[k], partner)
+    def held(i, c, o):
+        if i == 2:
+            return w_all.at[o]
+        return (x_all, dy_all)[i].at[rows(o), cols(c)]
+
+    def source(i, c):
+        if i == 2:
+            return w_in
+        return (x_in, dy_in)[i].at[:, cols(c)]
+
+    def origin(dev, k):
+        return lax.rem(dev + n - 4 * k, n)
+
+    def far(i, c, k):
+        return remote(
+            source(i, c), held(i, c, me), zsend.at[i, c, k], zrecv.at[i, c, k],
+            lax.rem(me + 4 * k, n),
+        )
+
+    def far_here(i, c, k):
+        dst = held(i, c, origin(me, k))
+        return remote(dst, dst, zsend.at[i, c, k], zrecv.at[i, c, k], lax.rem(me + 4 * k, n))
+
+    def over(i, c, k, dev, first=False):
+        dst = held(i, c, origin(dev, k))
+        return remote(
+            source(i, c) if first else dst, dst, xsend.at[i, c, k], xrecv.at[i, c, k], across
+        )
+
+    def pair(i, c, k, dev, first=False):
+        dst = held(i, c, origin(dev, k))
+        return remote(
+            source(i, c) if first else dst, dst, csend.at[i, c, k], crecv.at[i, c, k], partner
+        )
+
+    def pair_over(i, c, k, dev):
+        dst = held(i, c, origin(dev, k))
+        return remote(
+            dst, dst, csend.at[i, c, lines + k], crecv.at[i, c, lines + k], partner
+        )
+
+    def flip(dev):
+        return dev + 2 - 4 * lax.rem(dev // 2, 2)
+
+    def first_stage(c, kinds):
+        @pl.loop(1, lines)
+        def _(k):
+            for i in kinds:
+                far_here(i, c, k).wait_recv()
+                over(i, c, k, me).start()
+                pair(i, c, k, me).start()
+
+    def second_stage(c, kinds):
+        @pl.loop(0, lines)
+        def _(k):
+            for i in kinds:
+                over(i, c, k, across).wait_recv()
+                pair_over(i, c, k, across).start()
+
+    def third_stage(c, kinds):
+        @pl.loop(0, lines)
+        def _(k):
+            for i in kinds:
+                pair(i, c, k, partner).wait_recv()
+                pair_over(i, c, k, flip(partner)).wait_recv()
+
+    def begin(c, kinds):
+        for i in kinds:
+            over(i, c, 0, me, True).start()
+
+        @pl.loop(1, lines)
+        def _(k):
+            for i in kinds:
+                far(i, c, k).start()
+
+        for i in kinds:
+            pair(i, c, 0, me, True).start()
+
+    def finish(c, kinds):
+        for i in kinds:
+            over(i, c, 0, me, True).wait_send()
+            pair(i, c, 0, me, True).wait_send()
+            pair_over(i, c, 0, across).wait_send()
+
+        @pl.loop(1, lines)
+        def _(k):
+            for i in kinds:
+                far(i, c, k).wait_send()
+                over(i, c, k, me).wait_send()
+                pair(i, c, k, me).wait_send()
+                pair_over(i, c, k, across).wait_send()
 
     @pl.loop(0, chunks)
     def _(c):
-        for i in range(2):
-            pass_own(i, c).start()
-
-        @pl.loop(1, half)
-        def _(k):
-            for i in range(2):
-                send(i, c, k).start()
-
-    wpass_own().start()
-
-    @pl.loop(1, half)
-    def _(k):
-        wsend(k).start()
-
+        begin(c, (0, 1))
+
+    begin(0, (2,))
     acc[...] = jnp.zeros_like(acc)
     for copy in own:
         copy.wait()
+    first_stage(0, (0, 1))
+    second_stage(0, (0, 1))
+
+    def products(c, e):
+        for m in range(3):
+            slot = e * 3 + m
+            tile(c, e, m).wait()
+            acc[slot] += jnp.dot(
+                wbuf[slot], turned[m // 2], preferred_element_type=jnp.float32
+            )
+
+            @pl.when(c + 1 < chunks)
+            def _():
+                tile(c + 1, e, m).start()
 
     @pl.loop(0, chunks)
     def _(c):
-        @pl.loop(1, half)
-        def _(k):
-            for i in range(2):
-                arrive(i, c, k).wait_recv()
-                pass_on(i, c, k).start()
-
-        @pl.loop(0, half)
-        def _(k):
-            for i in range(2):
-                passed(i, c, k).wait_recv()
+        @pl.when(c + 1 < chunks)
+        def _():
+            first_stage(c + 1, (0, 1))
+
+        third_stage(c, (0, 1))
+        turned[0] = x_all[:, cols(c)].T
+        turned[1] = dy_all[:, cols(c)].T
 
         @pl.loop(0, experts)
         def _(e):
-            for m in range(3):
-                slot = e * 3 + m
-                tile(c, e, m).wait()
-                right = (x_all, x_all, dy_all)[m][:, cols(c)]
-                acc[slot] += lax.dot_general(
-                    wbuf[slot], right, (((1,), (1,)), ((), ())),
-                    preferred_element_type=jnp.float32,
-                )
-
-                @pl.when(c + 1 < chunks)
-                def _():
-                    tile(c + 1, e, m).start()
-
-    @pl.loop(1, half)
-    def _(k):
-        warrive(k).wait_recv()
-        wpass_on(k).start()
-
-    @pl.loop(0, half)
-    def _(k):
-        wpassed(k).wait_recv()
+            @pl.when((e == experts - 1) & (c + 1 < chunks))
+            def _():
+                second_stage(c + 1, (0, 1))
+
+            products(c, e)
+
+    first_stage(0, (2,))
+    second_stage(0, (2,))
+    third_stage(0, (2,))
 
     weights = jnp.sum(w_all[...], axis=0)
     strip = 32
@@ -190,21 +226,9 @@
 
     @pl.loop(0, chunks)
     def _(c):
-        for i in range(2):
-            pass_own(i, c).wait_send()
-
-        @pl.loop(1, half)
-        def _(k):
-            for i in range(2):
-                send(i, c, k).wait_send()
-                pass_on(i, c, k).wait_send()
-
-    wpass_own().wait_send()
-
-    @pl.loop(1, half)
-    def _(k):
-        wsend(k).wait_send()
-        wpass_on(k).wait_send()
+        finish(c, (0, 1))
+
+    finish(0, (2,))
 
 
 def grads_kernel(dg_t, du_t, aw_t, x, dy, out_g, out_u, out_d):
@@ -214,17 +238,19 @@
 
 def back_kernel(
     n, ne, dgu, sg, w_gate, w_up, out, gate_out,
-    wbuf, acc, part, rbuf, csum, gbuf, ebuf, s_r, s_c, s_g,
-    wsem, psend, precv, csend, crecv, esend, erecv,
+    wbuf, acc, part, rbuf, csum, xbuf, xsum, gbuf, ebuf, s_r, s_c, s_x, s_cx, s_g,
+    wsem, psend, precv, xsend, xrecv, csend, crecv, esend, erecv,
 ):
     experts, hidden, width = w_gate.shape
-    chunks, half = CHUNKS, n // 2
+    chunks, lines = BACK_CHUNKS, n // 4
     dc = width // chunks
     tb = out.shape[0]
     me, ep = lax.axis_index("blk"), lax.axis_index("ep")
     core = lax.rem(me, 2)
-    chip = me // 2
+    side = lax.rem(me // 2, 2)
+    line = me // 4
     partner = me + 1 - 2 * core
+    across = me + 2 - 4 * side
     mats = (w_gate, w_up)
     f32, bf16 = jnp.float32, jnp.bfloat16
 
@@ -247,10 +273,14 @@
     def to_partner(c):
         return remote(part.at[c, 1 - core], rbuf.at[c], psend.at[c], precv.at[c], blk=partner)
 
-    def to_chip(c, k):
-        q = lax.rem(chip + k, half)
-        return remote(
-            csum.at[c, rows(q)], gbuf.at[c, k], csend.at[c, k], crecv.at[c, k], blk=2 * q + core
+    def to_side(c):
+        return remote(csum.at[c, 1 - side], xbuf.at[c], xsend.at[c], xrecv.at[c], blk=across)
+
+    def to_line(c, k):
+        q = lax.rem(line + k, lines)
+        return remote(
+            xsum.at[c, rows(q)], gbuf.at[c, k], csend.at[c, k], crecv.at[c, k],
+            blk=4 * q + 2 * side + core,
         )
 
     def to_ep(c, k):
@@ -265,9 +295,15 @@
     def g_partner():
         return remote(sg, s_r, psend.at[chunks], precv.at[chunks], blk=partner)
 
-    def g_chip(k):
-        q = lax.rem(chip + k, half)
-        return remote(s_c, s_g.at[k], csend.at[chunks, k], crecv.at[chunks, k], blk=2 * q + core)
+    def g_side():
+        return remote(s_c, s_x, xsend.at[chunks], xrecv.at[chunks], blk=across)
+
+    def g_line(k):
+        q = lax.rem(line + k, lines)
+        return remote(
+            s_cx, s_g.at[k], csend.at[chunks, k], crecv.at[chunks, k],
+            blk=4 * q + 2 * side + core,
+        )
 
     def g_ep(k):
         return remote(
@@ -285,12 +321,12 @@
         for m in range(2):
             tile(0, e, m).start()
     greet(
-        [partner] + [lax.rem(me + 2 * k, n) for k in range(1, half)],
+        [partner, across] + [lax.rem(me + 4 * k, n) for k in range(1, lines)],
         [lax.rem(ep + k, ne) for k in range(1, ne)],
     )
     g_partner().start()
 
-    @pl.loop(0, chunks + 3)
+    @pl.loop(0, chunks + 4)
     def _(step):
         @pl.when(step < chunks)
         def _():
@@ -309,11 +345,13 @@
                     def _():
                         tile(c + 1, e, m).start()
 
-            for q in range(half):
-                for p in range(2):
-                    part[c, p, q * tb : (q + 1) * tb, :] = acc[
-                        (2 * q + p) * tb : (2 * q + p + 1) * tb, :
-                    ].astype(bf16)
+            for q in range(lines):
+                for x in range(2):
+                    for p in range(2):
+                        row = (4 * q + 2 * x + p) * tb
+                        part[c, p, x, q * tb : (q + 1) * tb, :] = acc[
+                            row : row + tb, :
+                        ].astype(bf16)
             to_partner(c).start()
 
         @pl.when((step >= 1) & (step < chunks + 1))
@@ -321,52 +359,65 @@
             c = step - 1
             to_partner(c).wait_recv()
             csum[c] = (part[c, core].astype(f32) + rbuf[c].astype(f32)).astype(bf16)
-
-            @pl.loop(1, half)
-            def _(k):
-                to_chip(c, k).start()
+            to_side(c).start()
 
         @pl.when(step == 1)
         def _():
             g_partner().wait_recv()
             s_c[...] = sg[...] + s_r[...]
-
-            @pl.loop(1, half)
+            g_side().start()
+
+        @pl.when((step >= 2) & (step < chunks + 2))
+        def _():
+            c = step - 2
+            to_side(c).wait_recv()
+            xsum[c] = (csum[c, side].astype(f32) + xbuf[c].astype(f32)).astype(bf16)
+
+            @pl.loop(1, lines)
             def _(k):
-                g_chip(k).start()
-
-        @pl.when((step >= 2) & (step < chunks + 2))
-        def _():
-            c = step - 2
-
-            @pl.loop(1, half)
+                to_line(c, k).start()
+
+        @pl.when(step == 2)
+        def _():
+            g_side().wait_recv()
+            s_cx[...] = s_c[...] + s_x[...]
+
+            @pl.loop(1, lines)
             def _(k):
-                to_chip(c, k).wait_recv()
-
-            total = csum[c, rows(chip)].astype(f32)
-            for k in range(1, half):
+                g_line(k).start()
+
+        @pl.when((step >= 3) & (step < chunks + 3))
+        def _():
+            c = step - 3
+
+            @pl.loop(1, lines)
+            def _(k):
+                to_line(c, k).wait_recv()
+
+            total = xsum[c, rows(line)].astype(f32)
+            for k in range(1, lines):
                 total = total + gbuf[c, k].astype(f32)
             ebuf[c, ep] = total.astype(bf16)
 
             for k in range(1, ne):
                 to_ep(c, k).start()
 
-        @pl.when(step == 2)
-        def _():
-            @pl.loop(1, half)
+        @pl.when(step == 3)
+        def _():
+            @pl.loop(1, lines)
             def _(k):
-                g_chip(k).wait_recv()
-
-            total = s_c[...]
-            for k in range(1, half):
+                g_line(k).wait_recv()
+
+            total = s_cx[...]
+            for k in range(1, lines):
                 total = total + s_g[k]
             gate_out[ep] = total
             for k in range(1, ne):
                 g_ep(k).start()
 
-        @pl.when(step >= 3)
-        def _():
-            c = step - 3
+        @pl.when(step >= 4)
+        def _():
+            c = step - 4
             for k in range(1, ne):
                 from_ep(c, k).wait_recv()
             total = ebuf[c, 0].astype(f32)
@@ -379,19 +430,22 @@
         g_ep(k).wait_send()
     g_partner().wait_send()
 
-    @pl.loop(1, half)
+    g_side().wait_send()
+
+    @pl.loop(1, lines)
     def _(k):
-        g_chip(k).wait_send()
+        g_line(k).wait_send()
 
     @pl.loop(0, chunks)
     def _(c):
         to_partner(c).wait_send()
+        to_side(c).wait_send()
         for k in range(1, ne):
             to_ep(c, k).wait_send()
 
-        @pl.loop(1, half)
+        @pl.loop(1, lines)
         def _(k):
-            to_chip(c, k).wait_send()
+            to_line(c, k).wait_send()
 
 
 def shards(n, ne, hidden_in, out_grad, expert_ids, gate_values, w_gate, w_up, w_down):
@@ -399,6 +453,7 @@
     experts, hidden, _ = w_gate.shape
     tokens, half, chunks = tb * n, n // 2, CHUNKS
     dc = width // chunks
+    back, bdc = BACK_CHUNKS, width // BACK_CHUNKS
     me, ep = lax.axis_index("blk"), lax.axis_index("ep")
     f32, bf16 = jnp.float32, jnp.bfloat16
     lines = -(-experts // 8) * 8
@@ -430,17 +485,16 @@
         scratch_shapes=[
             pltpu.VMEM((n, lines, tokens), f32),
             pltpu.VMEM((3 * experts, hidden, dc), bf16),
+            pltpu.VMEM((2, dc, tokens), bf16),
             pltpu.VMEM((3 * experts, hidden, tokens), f32),
             dma((3 * experts,)),
             dma((3,)),
-            dma((2, chunks, half)),
-            dma((2, chunks, half)),
-            dma((2, chunks, half)),
-            dma((2, chunks, half)),
-            dma((half,)),
-            dma((half,)),
-            dma((half,)),
-            dma((half,)),
+            dma((3, chunks, half // 2)),
+            dma((3, chunks, half // 2)),
+            dma((3, chunks, half // 2)),
+            dma((3, chunks, half // 2)),
+            dma((3, chunks, half)),
+            dma((3, chunks, half)),
         ],
         compiler_params=pltpu.CompilerParams(
             collective_id=0, has_side_effects=True, vmem_limit_bytes=VMEM_LIMIT
@@ -458,23 +512,29 @@
         in_specs=[vmem_spec, vmem_spec, any_spec, any_spec],
         out_specs=[vmem_spec] * 2,
         scratch_shapes=[
-            pltpu.VMEM((2 * experts, hidden, dc), bf16),
-            pltpu.VMEM((tokens, dc), f32),
-            pltpu.VMEM((chunks, 2, tokens // 2, dc), bf16),
-            pltpu.VMEM((chunks, tokens // 2, dc), bf16),
-            pltpu.VMEM((chunks, tokens // 2, dc), bf16),
-            pltpu.VMEM((chunks, half, tb, dc), bf16),
-            pltpu.VMEM((chunks, ne, tb, dc), bf16),
+            pltpu.VMEM((2 * experts, hidden, bdc), bf16),
+            pltpu.VMEM((tokens, bdc), f32),
+            pltpu.VMEM((back, 2, 2, tokens // 4, bdc), bf16),
+            pltpu.VMEM((back, 2, tokens // 4, bdc), bf16),
+            pltpu.VMEM((back, 2, tokens // 4, bdc), bf16),
+            pltpu.VMEM((back, tokens // 4, bdc), bf16),
+            pltpu.VMEM((back, tokens // 4, bdc), bf16),
+            pltpu.VMEM((back, n // 4, tb, bdc), bf16),
+            pltpu.VMEM((back, ne, tb, bdc), bf16),
             pltpu.VMEM((lines, tokens), f32),
             pltpu.VMEM((lines, tokens), f32),
-            pltpu.VMEM((half, lines, tokens), f32),
+            pltpu.VMEM((lines, tokens), f32),
+            pltpu.VMEM((lines, tokens), f32),
+            pltpu.VMEM((n // 4, lines, tokens), f32),
             dma((2 * experts,)),
-            dma((chunks + 1,)),
-            dma((chunks + 1,)),
-            dma((chunks + 1, half)),
-            dma((chunks + 1, half)),
-            dma((chunks + 1, ne)),
-            dma((chunks + 1, ne)),
+            dma((back + 1,)),
+            dma((back + 1,)),
+            dma((back + 1,)),
+            dma((back + 1,)),
+            dma((back + 1, n // 4)),
+            dma((back + 1, n // 4)),
+            dma((back + 1, ne)),
+            dma((back + 1, ne)),
         ],
         compiler_params=pltpu.CompilerParams(
             collective_id=1, has_side_effects=True, vmem_limit_bytes=VMEM_LIMIT

time: 145 us -> 138 us (0.952)
  Pallas kernels: 133 us -> 127 us
    pallas_call x1, Pallas kernels: 66.2 us -> 60.5 us  [shards(): pl.pallas_call(functools.partial(forward_kernel, n), out_shape=[jax.Shape...]
where the time goes in v1:
time: 138 us; the launch traced here: 137 us
  Pallas kernels  127 us (92%)
  local copies, waits for them, and re-layouts  6.3 us (5%)
  other arithmetic  3.46 us (3%)
    pallas_call x1, Pallas kernels, shards(): pl.pallas_call(functools.partial(forward_kernel, n), out_shape=[jax.Shape...  60.5 us
    pallas_call x1, Pallas kernels, shards(): pl.pallas_call(functools.partial(back_kernel, n, ne), out_shape=[jax.Shap...  43.5 us
    pallas_call x1, Pallas kernels, shards(): pl.pallas_call(grads_kernel, grid=(experts, width // wide), out_shape=[ja...  22.6 us
    pallas_call x2, local copies, waits for them, and re-layouts, shards(): pl.pallas_call(functools.partial(forward_kernel, n), out_shape=[jax.Shape...  3.06 us

profile of v1, /device:TPU:0, one launch (start us, length us, event | category | flops | bytes accessed | tf_op | source)
XLA Modules:
  0.0 137.1 jit_solution(13432216058916613714)
XLA Ops:
  0.6 0.8 slice_bitcast_fusion.1
  1.4 0.7 bitcast_convert_fusion.1
  2.1 0.1 select_add_fusion
  2.2 0.1 tile.10
  2.3 0.6 broadcast_select_fusion.w_in
  2.9 60.5 %gather_forward.1 = (bf16[256,4096]{1,0:T(8,128)(2,1)}, bf16[256,4096]{1,0:T(8,128)(2,1)}, bf16[2,896,256]{2,1,0:T(8,128)(2,1)}, bf16[2,896,256]{2,1,0:T(8,128)(...) custom-call(bf16[16,4096]{1,0:T(8,128)(2,1)} %x_in.1, bf16[16,4096]{1,0:T(8,128)(2,1)} %dy_in.1, ...), custom_call_target="tpu_custom_call" | custom-call | tf_op jit(solution)/shard_map/gather_forward/pallas_call | solution.py:473
  63.4 22.6 %weight_grads.1 = (bf16[2,896,4096]{2,1,0:T(8,128)(2,1)}, bf16[2,896,4096]{2,1,0:T(8,128)(2,1)}, bf16[2,896,4096]{2,1,0:T(8,128)(2,1)}) custom-call(bf16[2,896,256]{2,1,0:T(8,128)(2,1)} %get-tuple-element.16.dg_t, bf16[2,896,256]{2,1,0:T(8,128)(2,1)} %get-tuple-element.17.du_t, bf16[2,896,256]{2,1,0:T(8,128)(2,1)} %get-tuple-element.21.aw_t, ...), custom_call_target="tpu_custom_call" | custom-call | tf_op jit(solution)/shard_map/weight_grads/pallas_call | solution.py:549
  86.1 1.5 %copy.16 = bf16[2,896,256]{1,2,0:T(8,128)(2,1)S(1)} copy(bf16[2,896,256]{2,1,0:T(8,128)(2,1)} %get-tuple-element.16.dg_t) | data formatting | bytes 1835008 | tf_op jit(solution)/shard_map/gather_forward/pallas_call | solution.py:473
  87.6 1.5 %copy.17 = bf16[2,896,256]{1,2,0:T(8,128)(2,1)S(1)} copy(bf16[2,896,256]{2,1,0:T(8,128)(2,1)} %get-tuple-element.17.du_t) | data formatting | bytes 1835008 | tf_op jit(solution)/shard_map/gather_forward/pallas_call | solution.py:473
  89.2 1.4 %maximum_bitcast_fusion.dgu = bf16[2,2,256,896]{3,2,1,0:T(8,128)(2,1)} fusion(bf16[2,1,896,256]{2,3,1,0:T(8,128)(2,1)S(1)} %bitcast.17, bf16[2,1,896,256]{2,3,1,0:T(8,128)(2,1)S(1)} %bitcast.16), kind=kLoop, calls=%fused_computation | loop fusion | flops 917504 | bytes 3670016 | tf_op jit(solution)/shard_map/transpose | solution.py:505
  90.6 0.0 copy-start
  90.6 43.5 %back_scatter.1 = (bf16[16,4096]{1,0:T(8,128)(2,1)}, f32[2,8,256]{2,1,0:T(8,128)}) custom-call(bf16[2,2,256,896]{3,2,1,0:T(8,128)(2,1)} %maximum_bitcast_fusion.dgu, f32[8,256]{1,0:T(8,128)} %get-tuple-element.18.sg, bf16[2,896,4096]{2,1,0:T(8,128)(2,1)} %w_gate.3, bf16[2,896,4096]{2,1,0:T(8,128)(2,1)} %w_up.3), custom_call_target="tpu_custom_call" | custom-call | tf_op jit(solution)/shard_map/back_scatter/pallas_call | solution.py:506
  134.1 0.7 slice.19
  134.8 0.1 dynamic-slice_bitcast_fusion
  134.9 0.0 copy-done
  134.9 0.6 select_reduce_fusion
  135.5 1.6 %copy.19 = bf16[16,4096]{1,0:T(8,128)(2,1)} copy(bf16[16,4096]{1,0:T(8,128)(2,1)} %get-tuple-element.36) | data formatting | bytes 262144
  (5 shorter events, 0.0 us)
Async XLA Ops:
  90.6 44.3 %copy-start = (s32[16,2]{0,1:T(2,128)S(1)}, s32[16,2]{0,1:T(2,128)}, u32[]{:S(2)}) copy-start(s32[16,2]{0,1:T(2,128)} %param.9) | copy-start | bytes 388
